TPU v7x, 32 devices: a whole 2x2x4 slice. The times are simulated.
32 devices in a mesh: grp: 2 (over y), row: 4 (over x, core), col: 4 (over z).
Axes of the slice: x: 2, y: 2, z: 4, core: 2. Of those that a mesh axis runs over, the one named last changes fastest.
Arguments:
- factor: float32 [8, 4, 768, 768], P(('grp', 'row'), 'col'), parts along dimension 0
- rhs: float32 [8, 768, 64], P(('grp', 'row')), parts along dimension 0, may hold values from -6 to 6
- pattern: int32 [8, 4], P('grp'), parts along dimension 0, may hold values from 0 to 1, as said below
Outputs:
- solution: float32 [8, 768, 64], P(('grp', 'col'), 'row'), parts along dimension 0
There are 2 independent parts, one for each index of `grp`. A program takes and returns all parts, laid end to end along the dimension named above; each array names one. Nothing has to cross between parts.
Inputs may be any that keep to these rules, and one draw needn't show every extreme that they name: pattern[i, j] = 1 only where j < i; the blocks form an elimination tree in which every block but the last has exactly one parent p > j with pattern[p, j] = 1, and pattern[i, j] = 1 only where i is an ancestor of j; every chain of blocks linked by pattern has at most 4 blocks and some chain has exactly 4.
All inputs are finite; a program needn't handle non-finite values.
Results may differ from a plain program's by a relative error of at most 0.0001.
Values sent between devices are 32-bit elements; how exact they have to be, the bound alone decides.
A program may use at most 64 MiB of HBM per device.

v0:
```python
import jax
import jax.numpy as jnp
from jax import lax
from jax.sharding import PartitionSpec as P


def from_root(shard, axis, root):
    mine = lax.axis_index(axis) == root
    return lax.psum(jnp.where(mine, shard, jnp.zeros_like(shard)), axis)


def multiply(factor_tile, columns):
    return jnp.dot(
        factor_tile, columns, precision=lax.Precision.HIGHEST, preferred_element_type=jnp.float32
    )


def advance(factor_tile, right_cols, carried, solve_now, apply_now, final_level):

    def solve_branch(operand):
        return multiply(factor_tile, operand)

    def empty_branch(operand):
        return jnp.zeros_like(operand)

    fresh = lax.cond(solve_now, solve_branch, empty_branch, right_cols - carried)
    arrived = from_root(fresh, "row", lax.axis_index("col"))
    if not final_level:
        product = lax.cond(apply_now, solve_branch, empty_branch, arrived)
        carried = carried + lax.psum(product, "col")
    return (arrived, carried)


def local(factor, rhs, pattern):
    factor_tile = factor[0, 0]
    right_rows = rhs[0]
    here_row = lax.axis_index("row")
    here_col = lax.axis_index("col")
    depth_count = min(6, lax.axis_size("row"))
    linked = pattern == 1
    height = jnp.zeros((pattern.shape[0],), jnp.int32)
    for sweep_index in range(depth_count):
        height = jnp.max(jnp.where(linked, height[None, :] + 1, 0), axis=1)
    own_height = height[here_row]
    column_height = height[here_col]
    on_diagonal = here_row == here_col
    uses_block = pattern[here_row, here_col] == 1
    pieces = [right_rows]
    carried = [jnp.zeros_like(piece) for piece in pieces]
    solved = [jnp.zeros_like(piece) for piece in pieces]
    for level_now in range(depth_count):
        solve_now = on_diagonal & (own_height == level_now)
        apply_now = uses_block & (column_height == level_now)
        arrived, carried[0] = advance(
            factor_tile, pieces[0], carried[0], solve_now, apply_now, level_now == depth_count - 1
        )
        solved[0] = solved[0] + arrived
    solved_all = solved[0]
    own_rows = solved_all.shape[0] // lax.axis_size("row")
    return lax.dynamic_slice_in_dim(solved_all, here_row * own_rows, own_rows, 0)[None]


def solution(mesh):
    in_specs = (P(("grp", "row"), "col", None, None), P(("grp", "row"), None, None), P("grp", None))
    out_specs = P(("grp", "col"), "row", None)
    return jax.shard_map(local, mesh=mesh, in_specs=in_specs, out_specs=out_specs, check_vma=False)
```

profile of v0, /device:TPU:0, one launch (start us, length us, event | category | flops | bytes accessed | tf_op | source)
XLA Modules:
  0.0 278.0 jit_solution(16955222185634692702)
XLA Ops:
  6.5 0.0 all-reduce.8.cloned.1.call-start
  6.5 0.8 select_reduce_fusion.3
  7.3 0.1 select_reduce_fusion.2
  7.5 0.1 select_reduce_fusion.1
  7.6 0.1 select_reduce_fusion
  7.7 0.6 fusion.5
  9.0 1.1 copy.4
  10.1 3.8 %conditional.7 = (f32[768,64]{0,1:T(8,128)S(1)}) conditional(s32[]{:T(128)} %convert_element_type.21, () %tuple.47, (f32[768,768]{1,0:T(8,128)}, f32[768,64]{1,0:T(8,128)S(1)}) %tuple.101), branch_computations={%region_4.5_spmd, %region_5.6_spmd} | conditional | flops 452984832 | bytes 2752520 | solution.py:26
  10.1 3.8 %fusion.6 = f32[768,64]{0,1:T(8,128)S(1)} fusion(f32[768,768]{1,0:T(8,128)} %get-tuple-element.64, f32[768,64]{1,0:T(8,128)S(1)} %get-tuple-element.66), kind=kOutput, calls=%fused_computation.24 | convolution fusion | flops 452984832 | bytes 2752512 | tf_op jit(solution)/shard_map/cond/branch_1_fun/dot_general | solution.py:13
  13.9 0.7 broadcast_select_fusion.3
  14.6 0.0 all-reduce.8.cloned.1.call-update
  14.6 0.0 all-reduce.10.cloned.1.call-start
  14.6 1.3 dynamic_slice.13
  17.2 28.1 %all-reduce.8.cloned.1.call-done = f32[768,64]{0,1:T(8,128)} async-done(((f32[768,64]{0,1:T(8,128)}), f32[768,64]{0,1:T(8,128)}) %all-reduce.8.cloned.1.call-update) | async-done | bytes 196624 | tf_op jit(solution)/shard_map/psum | solution.py:9
  45.4 0.9 copy.6
  46.3 0.0 all-reduce.10.cloned.1.call-update
  46.3 0.0 all-reduce.12.cloned.1.call-start
  47.0 37.9 %all-reduce.10.cloned.1.call-done = f32[768,64]{1,0:T(8,128)} async-done(((f32[768,64]{1,0:T(8,128)}), f32[768,64]{1,0:T(8,128)}) %all-reduce.10.cloned.1.call-update) | async-done | bytes 196624 | tf_op jit(solution)/shard_map/psum | solution.py:30
  84.9 0.0 copy-start
  84.9 0.7 broadcast_select_fusion.2
  85.6 0.0 all-reduce.12.cloned.1.call-update
  85.7 0.0 all-reduce.14.cloned.1.call-start
  86.4 32.2 %all-reduce.12.cloned.1.call-done = f32[768,64]{0,1:T(8,128)} async-done(((f32[768,64]{0,1:T(8,128)}), f32[768,64]{0,1:T(8,128)}) %all-reduce.12.cloned.1.call-update) | async-done | bytes 196624 | tf_op jit(solution)/shard_map/psum | solution.py:9
  118.6 0.9 copy.8
  119.5 0.0 all-reduce.14.cloned.1.call-update
  119.5 0.0 all-reduce.16.cloned.1.call-start
  120.2 38.6 %all-reduce.14.cloned.1.call-done = f32[768,64]{1,0:T(8,128)} async-done(((f32[768,64]{1,0:T(8,128)}), f32[768,64]{1,0:T(8,128)}) %all-reduce.14.cloned.1.call-update) | async-done | bytes 196624 | tf_op jit(solution)/shard_map/psum | solution.py:30
  158.8 0.0 copy-done
  158.8 1.0 add.71
  159.9 0.7 broadcast_select_fusion.1
  160.6 0.0 all-reduce.16.cloned.1.call-update
  160.6 0.0 all-reduce.18.cloned.1.call-start
  161.3 34.4 %all-reduce.16.cloned.1.call-done = f32[768,64]{0,1:T(8,128)} async-done(((f32[768,64]{0,1:T(8,128)}), f32[768,64]{0,1:T(8,128)}) %all-reduce.16.cloned.1.call-update) | async-done | bytes 196624 | tf_op jit(solution)/shard_map/psum | solution.py:9
  195.7 0.2 conditional.12
  195.9 0.9 copy.10
  196.8 0.0 all-reduce.18.cloned.1.call-update
  196.9 0.0 all-reduce.20.cloned.1.call-start
  197.5 38.1 %all-reduce.18.cloned.1.call-done = f32[768,64]{1,0:T(8,128)} async-done(((f32[768,64]{1,0:T(8,128)}), f32[768,64]{1,0:T(8,128)}) %all-reduce.18.cloned.1.call-update) | async-done | bytes 196624 | tf_op jit(solution)/shard_map/psum | solution.py:30
  235.7 0.7 broadcast_select_fusion
  236.4 0.0 all-reduce.20.cloned.1.call-update
  236.4 32.9 %all-reduce.20.cloned.1.call-done = f32[768,64]{0,1:T(8,128)} async-done(((f32[768,64]{0,1:T(8,128)}), f32[768,64]{0,1:T(8,128)}) %all-reduce.20.cloned.1.call-update) | async-done | bytes 196624 | tf_op jit(solution)/shard_map/psum | solution.py:9
  269.3 1.8 fusion.4
  (14 shorter events, 0.2 us)
Async XLA Ops:
  6.5 38.8 %all-reduce.8.cloned.1.call-start = ((), (), s32[]{:S(2)}) async-start(), calls=%async_computation | async-start | bytes 393216 | tf_op jit(solution)/shard_map/psum | solution.py:9
  14.6 70.3 %all-reduce.10.cloned.1.call-start = ((), (), s32[]{:S(2)}) async-start(), calls=%async_computation.1 | async-start | bytes 786432 | tf_op jit(solution)/shard_map/psum | solution.py:30
  46.3 72.2 %all-reduce.12.cloned.1.call-start = ((), (), s32[]{:S(2)}) async-start(), calls=%async_computation.2 | async-start | bytes 393216 | tf_op jit(solution)/shard_map/psum | solution.py:9
  84.9 73.9 %copy-start = (f32[768,64]{1,0:T(8,128)S(1)}, f32[768,64]{1,0:T(8,128)}, u32[]{:S(2)}) copy-start(f32[768,64]{1,0:T(8,128)} %all-reduce.10.cloned.1.call-done) | copy-start | bytes 589828
  85.7 73.1 %all-reduce.14.cloned.1.call-start = ((), (), s32[]{:S(2)}) async-start(), calls=%async_computation.3 | async-start | bytes 786432 | tf_op jit(solution)/shard_map/psum | solution.py:30
  119.5 76.2 %all-reduce.16.cloned.1.call-start = ((), (), s32[]{:S(2)}) async-start(), calls=%async_computation.4 | async-start | bytes 393216 | tf_op jit(solution)/shard_map/psum | solution.py:9
  160.6 75.0 %all-reduce.18.cloned.1.call-start = ((), (), s32[]{:S(2)}) async-start(), calls=%async_computation.5 | async-start | bytes 786432 | tf_op jit(solution)/shard_map/psum | solution.py:30
  196.9 72.5 %all-reduce.20.cloned.1.call-start = ((), (), s32[]{:S(2)}) async-start(), calls=%async_computation.6 | async-start | bytes 393216 | tf_op jit(solution)/shard_map/psum | solution.py:9
Sparse Core Ops, SparseCore 0:
  14.7 30.5 all-reduce.7
  47.8 37.0 all-reduce.9
  87.2 31.2 all-reduce.11
  120.9 37.8 all-reduce.13
  161.0 34.6 all-reduce.15
  198.0 37.5 all-reduce.17
  238.0 31.2 all-reduce.19
where the time goes:
time: 278 us
  waiting for transfers between devices  242 us (87%)
  between operations  18.7 us (7%)
  other arithmetic  6.79 us (2%)
  local copies, waits for them, and re-layouts  5.85 us (2%)
  matrix products  3.79 us (1%)
    psum x4, waiting for transfers between devices, from_root(): return lax.psum(jnp.where(mine, shard, jnp.zeros_like(shard)), axis)  128 us
    psum x3, waiting for transfers between devices, advance(): carried = carried + lax.psum(product, 'col')  115 us
  transfers between devices with their start and end apart: 7, of which 7 were waited for; matrix products, arithmetic and copies ran while one was open for 0% of the time, Pallas kernels for 0%

commit v1 on v0

--- a/solution.py
+++ b/solution.py
@@ -2,6 +2,12 @@
 import jax.numpy as jnp
 from jax import lax
 from jax.sharding import PartitionSpec as P
+
+
+def summed_here(value, mesh_axis):
+    parts = lax.all_gather(value, mesh_axis, axis=0, tiled=False)
+    total = parts.sum(axis=0)
+    return total
 
 
 def from_root(shard, axis, root):
@@ -27,7 +33,7 @@
     arrived = from_root(fresh, "row", lax.axis_index("col"))
     if not final_level:
         product = lax.cond(apply_now, solve_branch, empty_branch, arrived)
-        carried = carried + lax.psum(product, "col")
+        carried = carried + summed_here(product, "col")
     return (arrived, carried)
 
 

time: 278 us -> 224 us (0.81)
  waiting for transfers between devices: 242 us -> 124 us
  blocking collectives: 0 us -> 57.1 us
  other arithmetic: 6.79 us -> 10.7 us
  local copies, waits for them, and re-layouts: 5.85 us -> 9.15 us
    psum x3 -> x0, waiting for transfers between devices: 115 us -> none  [advance(): carried = carried + lax.psum(product, 'col')]
    all_gather x0 -> x3, blocking collectives: none -> 57.1 us  [summed_here(): parts = lax.all_gather(value, mesh_axis, axis=0, tiled=False)]
    all_gather x0 -> x3, local copies, waits for them, and re-layouts: none -> 4.65 us  [summed_here(): parts = lax.all_gather(value, mesh_axis, axis=0, tiled=False)]
    psum x4, waiting for transfers between devices: 128 us -> 124 us  [from_root(): return lax.psum(jnp.where(mine, shard, jnp.zeros_like(shard)), axis)]
  transfers between devices with their start and end apart: 7 -> 4, of which waited for: 7 -> 4; matrix products, arithmetic and copies ran while one was open for 0% -> 1% of each run, Pallas kernels for 0% -> 0%
where the time goes in v1:
time: 224 us
  waiting for transfers between devices  124 us (55%)
  blocking collectives  57.1 us (25%)
  between operations  18.4 us (8%)
  other arithmetic  10.7 us (5%)
  local copies, waits for them, and re-layouts  9.15 us (4%)
  matrix products  3.79 us (2%)
    psum x4, waiting for transfers between devices, from_root(): return lax.psum(jnp.where(mine, shard, jnp.zeros_like(shard)), axis)  124 us
    all_gather x3, blocking collectives, summed_here(): parts = lax.all_gather(value, mesh_axis, axis=0, tiled=False)  57.1 us
    all_gather x3, local copies, waits for them, and re-layouts, summed_here(): parts = lax.all_gather(value, mesh_axis, axis=0, tiled=False)  4.65 us
  transfers between devices with their start and end apart: 4, of which 4 were waited for; matrix products, arithmetic and copies ran while one was open for 1% of the time, Pallas kernels for 0%

profile of v1, /device:TPU:0, one launch (start us, length us, event | category | flops | bytes accessed | tf_op | source)
XLA Modules:
  0.0 223.5 jit_solution(14867156561466725131)
XLA Ops:
  6.5 0.0 all-reduce.5.cloned.1.call-start
  6.5 0.8 select_reduce_fusion.3
  7.3 0.1 select_reduce_fusion.2
  7.5 0.1 select_reduce_fusion.1
  7.6 0.1 select_reduce_fusion
  7.7 0.7 fusion.5
  9.0 1.1 copy.9
  10.1 3.8 %conditional.7 = (f32[768,64]{0,1:T(8,128)S(1)}) conditional(s32[]{:T(128)} %convert_element_type.21, () %tuple.47, (f32[768,768]{1,0:T(8,128)}, f32[768,64]{1,0:T(8,128)S(1)}) %tuple.101), branch_computations={%region_4.5_spmd, %region_5.6_spmd} | conditional | flops 452984832 | bytes 2752520 | solution.py:32
  10.1 3.8 %fusion.6 = f32[768,64]{0,1:T(8,128)S(1)} fusion(f32[768,768]{1,0:T(8,128)} %get-tuple-element.68, f32[768,64]{1,0:T(8,128)S(1)} %get-tuple-element.69), kind=kOutput, calls=%fused_computation.24 | convolution fusion | flops 452984832 | bytes 2752512 | tf_op jit(solution)/shard_map/cond/branch_1_fun/dot_general | solution.py:19
  13.9 0.7 broadcast_select_fusion.3
  14.6 0.0 all-reduce.5.cloned.1.call-update
  14.6 0.0 all-reduce.7.cloned.1.call-start
  14.7 1.3 dynamic_slice.13
  17.9 27.4 %all-reduce.5.cloned.1.call-done = f32[768,64]{0,1:T(8,128)} async-done(((f32[768,64]{0,1:T(8,128)}), f32[768,64]{0,1:T(8,128)}) %all-reduce.5.cloned.1.call-update) | async-done | bytes 196624 | tf_op jit(solution)/shard_map/psum | solution.py:15
  45.4 0.0 copy-start
  45.4 17.9 %all-gather = f32[3072,64]{0,1:T(8,128)} all-gather(f32[768,64]{0,1:T(8,128)S(1)} %get-tuple-element.113), channel_id=2, replica_groups=mesh['grp'=2,'row'=4,'col'=4] {'col'}, dimensions={0}, use_global_device_ids=true | all-gather | bytes 983040 | tf_op jit(solution)/shard_map/all_gather | solution.py:8
  63.4 1.5 reshape.28
  64.9 1.2 reduce_sum.28
  66.1 0.0 copy-done
  66.1 0.7 broadcast_select_fusion.2
  66.8 0.0 all-reduce.7.cloned.1.call-update
  66.8 0.0 all-reduce.9.cloned.1.call-start
  68.1 31.9 %all-reduce.7.cloned.1.call-done = f32[768,64]{0,1:T(8,128)} async-done(((f32[768,64]{0,1:T(8,128)}), f32[768,64]{0,1:T(8,128)}) %all-reduce.7.cloned.1.call-update) | async-done | bytes 196624 | tf_op jit(solution)/shard_map/psum | solution.py:15
  100.1 19.4 %all-gather.1 = f32[3072,64]{0,1:T(8,128)} all-gather(f32[768,64]{0,1:T(8,128)S(1)} %get-tuple-element.115), channel_id=3, replica_groups=mesh['grp'=2,'row'=4,'col'=4] {'col'}, dimensions={0}, use_global_device_ids=true | all-gather | bytes 983040 | tf_op jit(solution)/shard_map/all_gather | solution.py:8
  119.5 1.5 reshape.29
  121.0 1.1 reduce_sum.29
  122.1 1.7 add.65
  123.9 0.2 conditional.11
  124.1 0.7 broadcast_select_fusion.1
  124.7 0.0 all-reduce.9.cloned.1.call-update
  124.8 0.0 all-reduce.11.cloned.1.call-start
  126.1 31.9 %all-reduce.9.cloned.1.call-done = f32[768,64]{0,1:T(8,128)} async-done(((f32[768,64]{0,1:T(8,128)}), f32[768,64]{0,1:T(8,128)}) %all-reduce.9.cloned.1.call-update) | async-done | bytes 196624 | tf_op jit(solution)/shard_map/psum | solution.py:15
  158.0 0.0 copy-start.1
  158.0 0.7 copy-done.1
  158.7 19.7 %all-gather.2 = f32[3072,64]{0,1:T(8,128)S(1)} all-gather(f32[768,64]{0,1:T(8,128)} %copy-done.1), channel_id=4, replica_groups=mesh['grp'=2,'row'=4,'col'=4] {'col'}, dimensions={0}, use_global_device_ids=true | all-gather | bytes 983040 | tf_op jit(solution)/shard_map/all_gather | solution.py:8
  178.4 1.6 copy.15
  180.0 0.7 conditional.13
  180.0 0.7 broadcast.44
  180.7 1.6 broadcast_select_fusion
  182.3 0.0 all-reduce.11.cloned.1.call-update
  182.4 32.8 %all-reduce.11.cloned.1.call-done = f32[768,64]{0,1:T(8,128)} async-done(((f32[768,64]{0,1:T(8,128)}), f32[768,64]{0,1:T(8,128)}) %all-reduce.11.cloned.1.call-update) | async-done | bytes 196624 | tf_op jit(solution)/shard_map/psum | solution.py:15
  215.2 1.8 fusion.4
  (12 shorter events, 0.2 us)
Async XLA Ops:
  6.5 38.9 %all-reduce.5.cloned.1.call-start = ((), (), s32[]{:S(2)}) async-start(), calls=%async_computation | async-start | bytes 393216 | tf_op jit(solution)/shard_map/psum | solution.py:15
  14.6 85.4 %all-reduce.7.cloned.1.call-start = ((), (), s32[]{:S(2)}) async-start(), calls=%async_computation.1 | async-start | bytes 393216 | tf_op jit(solution)/shard_map/psum | solution.py:15
  45.4 20.6 %copy-start = (f32[1,1,768,768]{3,2,1,0:T(8,128)S(1)}, f32[1,1,768,768]{3,2,1,0:T(8,128)}, u32[]{:S(2)}) copy-start(f32[1,1,768,768]{3,2,1,0:T(8,128)} %param.17) | copy-start | bytes 7077892
  66.8 91.2 %all-reduce.9.cloned.1.call-start = ((), (), s32[]{:S(2)}) async-start(), calls=%async_computation.2 | async-start | bytes 393216 | tf_op jit(solution)/shard_map/psum | solution.py:15
  124.8 90.4 %all-reduce.11.cloned.1.call-start = ((), (), s32[]{:S(2)}) async-start(), calls=%async_computation.3 | async-start | bytes 393216 | tf_op jit(solution)/shard_map/psum | solution.py:15
  158.0 0.7 copy-start.1
Sparse Core Ops, SparseCore 0:
  14.8 30.5 all-reduce.4
  66.9 33.0 all-reduce.6
  124.9 33.0 all-reduce.8
  182.5 32.6 all-reduce.10
